TPU v7x, 512 devices: a whole 4x8x8 slice. The times are simulated.
512 devices in a mesh: virt: 8 (over y), walk: 64 (over x, z, core).
Axes of the slice: x: 4, y: 8, z: 8, core: 2. Of those that a mesh axis runs over, the one named last changes fastest.
Arguments:
- inverse_rows: bfloat16 [64, 512, 2048], P('walk', None, 'virt'), may hold values from -3 to 3
- kinetic_rows: bfloat16 [64, 512, 2048], P('walk', None, 'virt'), may hold values from -1 to 1
- virt_values: bfloat16 [64, 2048, 4096], P('walk', None, 'virt'), may hold values from -6 to 6
- virt_laplacians: bfloat16 [64, 2048, 4096], P('walk', None, 'virt'), may hold values from -6 to 6
- local_energy: float32 [64], P('walk'), may hold values from 0.2 to 6, as said below
Outputs:
- energy_gradient: float32 [512, 4096], P('walk', 'virt')
- log_derivative_mean: float32 [512, 4096], P('walk', 'virt')
Inputs may be any that keep to these rules, and one draw needn't show every extreme that they name: `local_energy`: positive local energies.
All inputs are finite; a program needn't handle non-finite values.
Results may differ from a plain program's by a relative error of at most 0.0003.
Values may be sent and summed in bfloat16 or wider, within the bound.
A program may use at most 64 MiB of HBM per device.

v0:
```python
import jax
import jax.numpy as jnp
from jax import lax
from jax.sharding import PartitionSpec as P


def from_everyone(x, axis):
    devices = lax.axis_size(axis)
    return lax.all_to_all(jnp.broadcast_to(x[None], (devices, *x.shape)), axis, 0, 0, tiled=True)


def of_everyone(x, axis):
    everything = from_everyone(x, axis)
    return jnp.sum(everything, axis=0)


def side_by_side(arrays, axis, dim, along):
    both = jnp.concatenate(arrays, axis=along)
    out, at, gathered = (lax.all_gather(both, axis, axis=dim, tiled=True), 0, [])
    for a in arrays:
        gathered.append(lax.slice_in_dim(out, at, at + a.shape[along], axis=along))
        at += a.shape[along]
    return tuple(gathered)


def in_blocks(x, dim, devices):
    dims = x.shape
    blocks = x.reshape(*dims[:dim], devices, dims[dim] // devices, *dims[dim + 1 :])
    return jnp.moveaxis(blocks, dim, 0)


def sum_at_owner(x, axis, dim):
    devices = lax.axis_size(axis)
    blocks = lax.all_to_all(in_blocks(x, dim, devices), axis, 0, 0, tiled=True)
    return jnp.sum(blocks, axis=0)


def in_one_piece(arrays, axis, dim, along):
    widths = [a.shape[along] for a in arrays]
    both = jnp.concatenate(arrays, axis=along)
    out = sum_at_owner(both, axis, dim)
    return tuple(jnp.split(out, [sum(widths[:k]) for k in range(1, len(widths))], axis=along))


def product(left, right):
    return jnp.einsum("woe,wev->wov", left, right, preferred_element_type=jnp.float32)


def gradient_terms(log_grad, kin_part, weights):
    kin_grad = -0.5 * kin_part
    weighted = jnp.sum(weights[:, None, None] * log_grad + kin_grad, axis=0)
    return (weighted, jnp.sum(log_grad, axis=0))


def body(inverse_rows, kinetic_rows, virt_values, virt_laplacians, local_energy):
    walk_count = lax.axis_size("walk")
    walker_count = walk_count * local_energy.shape[0]
    energy_sum = of_everyone(jnp.sum(local_energy), "walk")
    average = energy_sum / walker_count
    weights = 2.0 * (local_energy - average)
    inverse_all, kinetic_all = side_by_side((inverse_rows, kinetic_rows), "virt", 2, 0)
    log_grad = product(inverse_all, virt_values)
    kin_part = product(inverse_all, virt_laplacians) - product(kinetic_all, virt_values)
    weighted, log_sum = gradient_terms(log_grad, kin_part, weights)
    summed = in_one_piece((weighted, log_sum), "walk", 0, 1)
    gradient_part, log_part = (summed[0], summed[1])
    return (gradient_part / walker_count, log_part / walker_count)


def solution(mesh):
    placed = (
        P("walk", None, "virt"),
        P("walk", None, "virt"),
        P("walk", None, "virt"),
        P("walk", None, "virt"),
        P("walk"),
    )
    return jax.shard_map(
        body,
        mesh=mesh,
        in_specs=placed,
        out_specs=(P("walk", "virt"), P("walk", "virt")),
        check_vma=False,
    )
```

profile of v0, /device:TPU:1, one launch (start us, length us, event | category | flops | bytes accessed | tf_op | source)
XLA Modules:
  0.0 158.4 jit_solution(4874859541301332890)
XLA Ops:
  7.2 0.0 copy-start
  7.2 0.0 all-gather.2.cloned.1.call-start
  7.2 2.0 %pad_maximum_fusion.1 = bf16[2,512,256]{2,1,0:T(8,128)(2,1)} fusion(bf16[1,512,256]{2,1,0:T(8,128)(2,1)} %param.6, bf16[1,512,256]{2,1,0:T(8,128)(2,1)} %param.5), kind=kLoop, calls=%fused_computation.13 | loop fusion | flops 262144 | bytes 1048576 | tf_op jit(solution)/shard_map/concatenate | solution.py:18
  9.2 0.0 all-gather.2.cloned.1.call-update
  9.9 23.9 %all_to_all.11 = f32[64,1,1]{2,1,0:T(1,128)S(1)} all-to-all(f32[64,1,1]{2,1,0:T(1,128)S(1)} %broadcast_in_dim.10), channel_id=1, replica_groups=mesh['virt'=8,'walk'=64] {'walk'}, dimensions={0} | all-to-all | bytes 512 | tf_op jit(solution)/shard_map/all_to_all | solution.py:9
  33.9 0.7 reduce_sum.16
  35.2 41.3 %all-gather.2.cloned.1.call-done = bf16[2,512,2048]{2,1,0:T(8,128)(2,1)} async-done(((bf16[2,512,256]{2,1,0:T(8,128)(2,1)}), bf16[2,512,2048]{2,1,0:T(8,128)(2,1)}) %all-gather.2.cloned.1.call-update) | async-done | bytes 4194320 | tf_op jit(solution)/shard_map/all_gather | solution.py:19
  76.5 0.0 copy-done
  76.5 0.0 copy-start.1
  76.5 3.0 %fusion.4 = f32[512,512]{1,0:T(8,128)S(1)} fusion(bf16[1,2048,512]{2,1,0:T(8,128)(2,1)S(1)} %copy-done, bf16[2,512,2048]{2,1,0:T(8,128)(2,1)} %all-gather.2.cloned.1.call-done), kind=kOutput, calls=%fused_computation.7 | convolution fusion | flops 1073741824 | bytes 5242880 | tf_op jit(solution)/shard_map/woe,wev->wov/dot_general | solution.py:46
  79.5 0.0 copy-done.1
  79.5 0.0 copy-start.2
  79.5 1.2 fusion
  80.8 0.3 copy-done.2
  81.1 1.3 fusion.15
  82.4 0.2 pad_maximum_fusion
  82.6 66.6 %all_to_all.12 = f32[64,8,1024]{2,1,0:T(8,128)} all-to-all(f32[64,8,1024]{2,1,0:T(8,128)S(1)} %pad_maximum_fusion), channel_id=1, replica_groups=mesh['virt'=8,'walk'=64] {'walk'}, dimensions={0} | all-to-all | bytes 4194304 | tf_op jit(solution)/shard_map/all_to_all | solution.py:34
  149.2 1.7 %reduce_sum.20 = f32[8,1024]{1,0:T(8,128)S(1)} reduce(f32[64,8,1024]{2,1,0:T(8,128)} %all_to_all.12, f32[]{:T(128)} %constant.4.clone.1), dimensions={0}, to_apply=%region_1.0 | reduce | flops 516096 | bytes 2129924 | tf_op jit(solution)/shard_map/reduce_sum | solution.py:35
  150.9 0.6 slice_multiply_fusion
  (1 shorter events, 0.0 us)
Async XLA Ops:
  7.2 69.4 %copy-start = (bf16[1,2048,512]{2,1,0:T(8,128)(2,1)S(1)}, bf16[1,2048,512]{2,1,0:T(8,128)(2,1)}, u32[]{:S(2)}) copy-start(bf16[1,2048,512]{2,1,0:T(8,128)(2,1)} %param.7) | copy-start | bytes 6291460
  7.2 69.3 %all-gather.2.cloned.1.call-start = ((), (), s32[]{:S(2)}) async-start(), calls=%async_computation.2 | async-start | bytes 4718592 | tf_op jit(solution)/shard_map/all_gather | solution.py:19
  76.5 3.0 %copy-start.1 = (bf16[2,512,2048]{2,1,0:T(8,128)(2,1)S(1)}, bf16[2,512,2048]{2,1,0:T(8,128)(2,1)}, u32[]{:S(2)}) copy-start(bf16[2,512,2048]{2,1,0:T(8,128)(2,1)} %all-gather.2.cloned.1.call-done) | copy-start | bytes 12582916
  79.5 1.6 %copy-start.2 = (bf16[1,2048,512]{2,1,0:T(8,128)(2,1)S(1)}, bf16[1,2048,512]{2,1,0:T(8,128)(2,1)}, u32[]{:S(2)}) copy-start(bf16[1,2048,512]{2,1,0:T(8,128)(2,1)} %param.8) | copy-start | bytes 6291460
Sparse Core Ops, SparseCore 0:
  10.0 66.4 all-gather.1
where the time goes:
time: 159 us; the launch traced here: 158 us
  blocking collectives  90.6 us (57%)
  waiting for transfers between devices  41.3 us (26%)
  between operations  15.4 us (10%)
  matrix products  5.49 us (3%)
  other arithmetic  5.21 us (3%)
    all_to_all x1, blocking collectives, sum_at_owner(): blocks = lax.all_to_all(in_blocks(x, dim, devices), axis, 0, 0, tiled=True)  66.6 us
    all_gather x1, waiting for transfers between devices, side_by_side(): lax.all_gather(both, axis, axis=dim, tiled=True)  41.3 us
    all_to_all x1, blocking collectives, from_everyone(): lax.all_to_all(jnp.broadcast_to(x[None], (devices, *x.shape)), axis, 0, 0...  23.9 us
    dot_general x3, matrix products, product(): jnp.einsum('woe,wev->wov', left, right, preferred_element_type=jnp.float32)  5.49 us
  transfers between devices with their start and end apart: 1, of which 1 were waited for; matrix products, arithmetic and copies ran while one was open for 0% of the time, Pallas kernels for 0%

commit v1 on v0

v1 whole, which is shorter than its diff:
```python
import functools

import jax
import jax.numpy as jnp
from jax import lax
from jax.experimental import pallas as pl
from jax.experimental.pallas import tpu as pltpu
from jax.sharding import PartitionSpec as P

MESH = pl.DeviceIdType.MESH
X, Z, CORES = 4, 8, 2
GROUP = X * CORES
OWN, RIGHT, LEFT, FAR = 0, 1, 4, 7


def kernel(sizes, inverse, kinetic, values, laplacians, energy, gradient, log_mean, *scratch):
    ring, occ, depth, cols, chunks, rows = sizes
    (raw, wide, held, vals, laps, acc, acc_lap, part, part_in, row, row_in, done) = scratch[:12]
    (e_own, e_in, e_sum, e_sum_in) = scratch[12:16]
    (load_sem, ring_send, ring_recv, part_send, part_recv, row_send, row_recv, e_send, e_recv) = scratch[16:]
    walkers = X * Z * CORES

    y = lax.axis_index("virt")
    w = lax.axis_index("walk")
    x, z, core = w // (Z * CORES), (w // CORES) % Z, w % CORES
    group = x * CORES + core
    right, left = lax.rem(y + 1, ring), lax.rem(y + ring - 1, ring)

    def in_group(i):
        other = lax.rem(group + i, GROUP)
        return other, {"walk": ((other // CORES) * Z + z) * CORES + other % CORES}

    def along_z(i):
        other = lax.rem(z + i, Z)
        return other, {"walk": (x * Z + other) * CORES + core}

    loads = [
        pltpu.make_async_copy(inverse.at[0], raw.at[0], load_sem.at[0]),
        pltpu.make_async_copy(kinetic.at[0], raw.at[1], load_sem.at[1]),
        pltpu.make_async_copy(values.at[0], vals, load_sem.at[2]),
        pltpu.make_async_copy(laplacians.at[0], laps, load_sem.at[3]),
    ]
    for load in loads:
        load.start()

    barrier = pltpu.get_barrier_semaphore()
    for to in (right, left):
        pl.semaphore_signal(barrier, inc=1, device_id={"virt": to}, device_id_type=MESH)
    for i in range(1, GROUP):
        pl.semaphore_signal(barrier, inc=1, device_id=in_group(i)[1], device_id_type=MESH)
    for i in range(1, Z):
        pl.semaphore_signal(barrier, inc=1, device_id=along_z(i)[1], device_id_type=MESH)

    def hop(j, way, step):
        base = RIGHT if way == 0 else LEFT
        if step == 3:
            src, dst = held.at[j, base + 2, way], held.at[j, FAR, way]
        else:
            src = held.at[j, OWN if step == 0 else base + step - 1]
            dst = held.at[j, base + step]
        return pltpu.make_async_remote_copy(
            src_ref=src,
            dst_ref=dst,
            send_sem=ring_send.at[way, step],
            recv_sem=ring_recv.at[way, step, j],
            device_id={"virt": right if way == 0 else left},
            device_id_type=MESH,
        )

    def permute(j):
        for a in range(2):
            for half in range(depth // 128):
                pieces = [
                    wide[a, half, pl.ds(Z * CORES * chunks * (g // CORES) + chunks * (g % CORES) + j, Z, stride=CORES * chunks), :]
                    for g in range(GROUP)
                ]
                held[j, OWN, a, :, half * 128 : (half + 1) * 128] = jnp.concatenate(pieces, axis=0).astype(held.dtype)

    for a in range(2):
        loads[a].wait()
        for half in range(depth // 128):
            wide[a, half] = raw[a, :, half * 128 : (half + 1) * 128].astype(jnp.float32)
    permute(0)
    e_own[...] = jnp.full(e_own.shape, energy[0], jnp.float32)
    pl.semaphore_wait(barrier, 2 + (GROUP - 1) + (Z - 1))
    for j in range(2):
        if j:
            permute(j)
        for way in range(2):
            hop(j, way, 0).start()
    for i in range(1, GROUP):
        pltpu.make_async_remote_copy(
            src_ref=e_own, dst_ref=e_in.at[i - 1], send_sem=e_send.at[0], recv_sem=e_recv.at[0],
            device_id=in_group(i)[1], device_id_type=MESH,
        ).start()
    for j in range(2, chunks):
        permute(j)
    for load in loads[2:]:
        load.wait()

    def accumulate(j, slot, origin, first=False):
        at = pl.ds(pl.multiple_of(origin * depth, depth), depth)
        both = held[j, slot].reshape(2 * rows, depth)
        mine = jnp.dot(both, vals[at, :], preferred_element_type=jnp.float32)
        curved = jnp.dot(both[:rows], laps[at, :], preferred_element_type=jnp.float32)
        if first:
            acc[j] = mine
            acc_lap[j] = curved
        else:
            acc[j] += mine
            acc_lap[j] += curved

    def send_part(j):
        log_grad = acc[j, :rows]
        kin_part = acc_lap[j] - acc[j, rows:]
        weighted = 2.0 * energy[0] * log_grad - 0.5 * kin_part
        part[j, :, :, :cols] = weighted.reshape(GROUP, Z, cols)
        part[j, :, :, cols:] = log_grad.reshape(GROUP, Z, cols)
        for i in range(1, GROUP):
            other, device = in_group(i)
            pltpu.make_async_remote_copy(
                src_ref=part.at[j, other], dst_ref=part_in.at[j, i - 1], send_sem=part_send, recv_sem=part_recv.at[j],
                device_id=device, device_id_type=MESH,
            ).start()

    def wait_bytes(ref, sem):
        pltpu.make_async_copy(ref, ref, sem).wait()

    def send_rows(j):
        wait_bytes(part_in.at[j], part_recv.at[j])
        total = part[j, group]
        for i in range(GROUP - 1):
            total = total + part_in[j, i]
        lanes = 2 * cols // Z
        for c in range(Z):
            row[j, pl.ds(c, Z, stride=Z), :] = total[:, c * lanes : (c + 1) * lanes]
        for i in range(1, Z):
            other, device = along_z(i)
            pltpu.make_async_remote_copy(
                src_ref=row.at[j, pl.ds(pl.multiple_of(other * Z, Z), Z)], dst_ref=row_in.at[j, i - 1],
                send_sem=row_send, recv_sem=row_recv.at[j], device_id=device, device_id_type=MESH,
            ).start()

    def finish(j):
        wait_bytes(row_in.at[j], row_recv.at[j])
        total = row[j, pl.ds(pl.multiple_of(z * Z, Z), Z)]
        for i in range(Z - 1):
            total = total + row_in[j, i]
        done[pl.ds(pl.multiple_of(j * Z, Z), Z), :] = total

    def within(j):
        return jnp.logical_and(j >= 0, j < chunks)

    def one_round(r, carry):
        @pl.when(r + 2 < chunks)
        def _():
            for way in range(2):
                hop(r + 2, way, 0).start()

        for step in range(1, 4):
            j = r - step + 1

            @pl.when(within(j))
            def _():
                for way in range(2):
                    hop(j, way, step - 1).wait_recv()
                    hop(j, way, step).start()

        far = r - 3

        @pl.when(within(far))
        def _():
            for way in range(2):
                hop(far, way, 3).wait_recv()
            accumulate(far, FAR, lax.rem(y + 4, ring))
            send_part(far)

        @pl.when(within(r))
        def _():
            accumulate(r, OWN, y, first=True)

        for step in range(1, 4):
            j = r - step + 1

            @pl.when(within(j))
            def _():
                accumulate(j, RIGHT + step - 1, lax.rem(y + ring - step, ring))
                accumulate(j, LEFT + step - 1, lax.rem(y + step, ring))

        @pl.when(r == 2)
        def _():
            wait_bytes(e_in, e_recv.at[0])
            total = e_own[...]
            for i in range(GROUP - 1):
                total = total + e_in[i]
            e_sum[...] = total
            for i in range(1, Z):
                pltpu.make_async_remote_copy(
                    src_ref=e_sum, dst_ref=e_sum_in.at[i - 1], send_sem=e_send.at[1], recv_sem=e_recv.at[1],
                    device_id=along_z(i)[1], device_id_type=MESH,
                ).start()

        @pl.when(within(r - 5))
        def _():
            send_rows(r - 5)

        @pl.when(within(r - 6))
        def _():
            finish(r - 6)

        return carry

    lax.fori_loop(0, chunks + 6, one_round, 0)

    wait_bytes(e_sum_in, e_recv.at[1])
    e_total = e_sum[...]
    for i in range(Z - 1):
        e_total = e_total + e_sum_in[i]
    average = e_total / walkers
    lanes = 2 * cols // Z
    for c in range(Z // 2):
        weighted = done[pl.ds(c, chunks, stride=Z), :] / walkers
        logs = done[pl.ds(c + Z // 2, chunks, stride=Z), :] / walkers
        gradient[:, c * lanes : (c + 1) * lanes] = weighted - 2.0 * average * logs
        log_mean[:, c * lanes : (c + 1) * lanes] = logs

    for way in range(2):
        base = RIGHT if way == 0 else LEFT
        for step in range(3):
            wait_bytes(held.at[:, base + step], ring_send.at[way, step])
        wait_bytes(held.at[:, FAR, way], ring_send.at[way, 3])
    wait_bytes(part_in, part_send)
    wait_bytes(row_in, row_send)
    wait_bytes(e_in, e_send.at[0])
    wait_bytes(e_sum_in, e_send.at[1])


def body(inverse_rows, kinetic_rows, virt_values, virt_laplacians, local_energy):
    ring = lax.axis_size("virt")
    walkers = lax.axis_size("walk")
    _, occ, depth = inverse_rows.shape
    _, electrons, cols = virt_values.shape
    chunks = occ // walkers
    rows = walkers
    sizes = (ring, occ, depth, cols, chunks, rows)
    hbm = pl.BlockSpec(memory_space=pl.ANY)
    vmem = pl.BlockSpec(memory_space=pltpu.VMEM)
    f32, b16 = jnp.float32, inverse_rows.dtype
    dma = pltpu.SemaphoreType.DMA
    lanes = 2 * cols // Z
    out = jax.ShapeDtypeStruct((occ // walkers, cols), f32)
    return pl.pallas_call(
        functools.partial(kernel, sizes),
        out_shape=(out, out),
        in_specs=[hbm, hbm, hbm, hbm, pl.BlockSpec(memory_space=pltpu.SMEM)],
        out_specs=(vmem, vmem),
        scratch_shapes=[
            pltpu.VMEM((2, occ, depth), b16),
            pltpu.VMEM((2, depth // 128, occ, 128), f32),
            pltpu.VMEM((chunks, ring, 2, rows, depth), b16),
            pltpu.VMEM((electrons, cols), b16),
            pltpu.VMEM((electrons, cols), b16),
            pltpu.VMEM((chunks, 2 * rows, cols), f32),
            pltpu.VMEM((chunks, rows, cols), f32),
            pltpu.VMEM((chunks, GROUP, Z, 2 * cols), f32),
            pltpu.VMEM((chunks, GROUP - 1, Z, 2 * cols), f32),
            pltpu.VMEM((chunks, Z * Z, lanes), f32),
            pltpu.VMEM((chunks, Z - 1, Z, lanes), f32),
            pltpu.VMEM((chunks * Z, lanes), f32),
            pltpu.VMEM((8, lanes), f32),
            pltpu.VMEM((GROUP - 1, 8, lanes), f32),
            pltpu.VMEM((8, lanes), f32),
            pltpu.VMEM((Z - 1, 8, lanes), f32),
            dma((4,)),
            dma((2, 4)),
            dma((2, 4, chunks)),
            dma,
            dma((chunks,)),
            dma,
            dma((chunks,)),
            dma((2,)),
            dma((2,)),
        ],
        compiler_params=pltpu.CompilerParams(collective_id=0, has_side_effects=True, vmem_limit_bytes=56 * 1024 * 1024),
    )(inverse_rows, kinetic_rows, virt_values, virt_laplacians, local_energy)


def solution(mesh):
    placed = (
        P("walk", None, "virt"),
        P("walk", None, "virt"),
        P("walk", None, "virt"),
        P("walk", None, "virt"),
        P("walk"),
    )
    return jax.shard_map(
        body,
        mesh=mesh,
        in_specs=placed,
        out_specs=(P("walk", "virt"), P("walk", "virt")),
        check_vma=False,
    )
```

time: 159 us -> 74.5 us (0.47)
  blocking collectives: 90.6 us -> 0 us
  Pallas kernels: 0 us -> 70.2 us
  waiting for transfers between devices: 41.3 us -> 0 us
  between operations: 15.4 us -> 1.29 us
  matrix products: 5.49 us -> 0 us
  other arithmetic: 5.21 us -> 0 us
  local copies, waits for them, and re-layouts: 0.37 us -> 2.65 us
    all_to_all x2 -> x0, blocking collectives: 90.6 us -> none  [the longest x1 66.6 us: sum_at_owner(): blocks = lax.all_to_all(in_blocks(x, dim, devices), axis, 0, 0, tiled=True)]
    pallas_call x0 -> x1, Pallas kernels: none -> 70.2 us  [body(): pl.pallas_call(functools.partial(kernel, sizes), out_shape=(out, out), in...]
    all_gather x1 -> x0, waiting for transfers between devices: 41.3 us -> none  [side_by_side(): lax.all_gather(both, axis, axis=dim, tiled=True)]
    dot_general x3 -> x0, matrix products: 5.49 us -> none  [product(): jnp.einsum('woe,wev->wov', left, right, preferred_element_type=jnp.float32)]
    reduce_sum x2 -> x0, other arithmetic: 2.4 us -> none  [the longest x1 1.73 us: sum_at_owner(): return jnp.sum(blocks, axis=0)]
    unnamed x6 -> x2, local copies, waits for them, and re-layouts: 0.35 us -> 2.65 us
    concatenate x2 -> x0, other arithmetic: 2.19 us -> none  [the longest x1 2.01 us: side_by_side(): both = jnp.concatenate(arrays, axis=along)]
  transfers between devices with their start and end apart: 1 -> 0, of which waited for: 1 -> 0; matrix products, arithmetic and copies ran while one was open for 0% -> 0% of each run, Pallas kernels for 0% -> 0%
where the time goes in v1:
time: 74.5 us; the launch traced here: 74.2 us
  Pallas kernels  70.2 us (94%)
  local copies, waits for them, and re-layouts  2.65 us (4%)
  between operations  1.29 us (2%)
    pallas_call x1, Pallas kernels, body(): pl.pallas_call(functools.partial(kernel, sizes), out_shape=(out, out), in...  70.2 us
    unnamed x2, local copies, waits for them, and re-layouts  2.65 us

profile of v1, /device:TPU:1, one launch (start us, length us, event | category | flops | bytes accessed | tf_op | source)
XLA Modules:
  0.0 74.2 jit_solution(16144918671413422891)
XLA Ops:
  1.3 70.2 %shard_map.68 = (f32[8,512]{1,0:T(8,128)}, f32[8,512]{1,0:T(8,128)}) custom-call(bf16[1,512,256]{2,1,0:T(8,128)(2,1)} %inverse.1, bf16[1,512,256]{2,1,0:T(8,128)(2,1)} %kinetic.1, bf16[1,2048,512]{2,1,0:T(8,128)(2,1)} %values.1, bf16[1,2048,512]{2,1,0:T(8,128)(2,1)} %laplacians.1, f32[1]{0:T(128)S(6)} %copy.9.energy), custom_call_target="tpu_custom_call" | custom-call | tf_op jit(solution)/shard_map/pallas_call | solution.py:252
  71.5 1.3 %copy.10 = f32[8,512]{1,0:T(8,128)} copy(f32[8,512]{1,0:T(8,128)} %get-tuple-element.4) | data formatting | bytes 32768
  72.9 1.3 %copy.11 = f32[8,512]{1,0:T(8,128)} copy(f32[8,512]{1,0:T(8,128)} %get-tuple-element.5) | data formatting | bytes 32768

commit v2 on v1

--- a/solution.py
+++ b/solution.py
@@ -13,11 +13,11 @@
 OWN, RIGHT, LEFT, FAR = 0, 1, 4, 7
 
 
-def kernel(sizes, inverse, kinetic, values, laplacians, energy, gradient, log_mean, *scratch):
+def kernel(sizes, inverse, kinetic, values, laplacians, energy_in, sums, *scratch):
     ring, occ, depth, cols, chunks, rows = sizes
     (raw, wide, held, vals, laps, acc, acc_lap, part, part_in, row, row_in, done) = scratch[:12]
-    (e_own, e_in, e_sum, e_sum_in) = scratch[12:16]
-    (load_sem, ring_send, ring_recv, part_send, part_recv, row_send, row_recv, e_send, e_recv) = scratch[16:]
+    (e_own, e_in, e_sum, e_sum_in, energy) = scratch[12:17]
+    (load_sem, ring_send, ring_recv, part_send, part_recv, row_send, row_recv, e_send, e_recv, known) = scratch[17:]
     walkers = X * Z * CORES
 
     y = lax.axis_index("virt")
@@ -39,17 +39,24 @@
         pltpu.make_async_copy(kinetic.at[0], raw.at[1], load_sem.at[1]),
         pltpu.make_async_copy(values.at[0], vals, load_sem.at[2]),
         pltpu.make_async_copy(laplacians.at[0], laps, load_sem.at[3]),
+        pltpu.make_async_copy(energy_in, energy, load_sem.at[4]),
     ]
     for load in loads:
         load.start()
 
     barrier = pltpu.get_barrier_semaphore()
-    for to in (right, left):
-        pl.semaphore_signal(barrier, inc=1, device_id={"virt": to}, device_id_type=MESH)
-    for i in range(1, GROUP):
-        pl.semaphore_signal(barrier, inc=1, device_id=in_group(i)[1], device_id_type=MESH)
-    for i in range(1, Z):
-        pl.semaphore_signal(barrier, inc=1, device_id=along_z(i)[1], device_id_type=MESH)
+    near = [{"walk": ((lax.rem(x + d, X)) * Z + z) * CORES + core} for d in (1, X - 1)]
+    near += [{"walk": (x * Z + lax.rem(z + d, Z)) * CORES + core} for d in (1, Z - 1)]
+    near += [{"walk": (x * Z + z) * CORES + 1 - core}]
+    for device in near + [{"virt": right}, {"virt": left}]:
+        pl.semaphore_signal(barrier, inc=1, device_id=device, device_id_type=MESH)
+
+    def tell(stage):
+        for device in near:
+            pl.semaphore_signal(known.at[stage], inc=1, device_id=device, device_id_type=MESH)
+
+    def learn(stage):
+        pl.semaphore_wait(known.at[stage], len(near))
 
     def hop(j, way, step):
         base = RIGHT if way == 0 else LEFT
@@ -81,21 +88,18 @@
         for half in range(depth // 128):
             wide[a, half] = raw[a, :, half * 128 : (half + 1) * 128].astype(jnp.float32)
     permute(0)
-    e_own[...] = jnp.full(e_own.shape, energy[0], jnp.float32)
-    pl.semaphore_wait(barrier, 2 + (GROUP - 1) + (Z - 1))
+    pl.semaphore_wait(barrier, len(near) + 2)
     for j in range(2):
         if j:
             permute(j)
         for way in range(2):
             hop(j, way, 0).start()
-    for i in range(1, GROUP):
-        pltpu.make_async_remote_copy(
-            src_ref=e_own, dst_ref=e_in.at[i - 1], send_sem=e_send.at[0], recv_sem=e_recv.at[0],
-            device_id=in_group(i)[1], device_id_type=MESH,
-        ).start()
+    tell(0)
+    loads[4].wait()
+    e_own[...] = jnp.full(e_own.shape, energy[0], jnp.float32)
     for j in range(2, chunks):
         permute(j)
-    for load in loads[2:]:
+    for load in loads[2:4]:
         load.wait()
 
     def accumulate(j, slot, origin, first=False):
@@ -187,7 +191,26 @@
                 accumulate(j, RIGHT + step - 1, lax.rem(y + ring - step, ring))
                 accumulate(j, LEFT + step - 1, lax.rem(y + step, ring))
 
+        @pl.when(r == 0)
+        def _():
+            learn(0)
+            tell(1)
+
+        @pl.when(r == 1)
+        def _():
+            learn(1)
+            tell(2)
+            for i in range(1, GROUP):
+                pltpu.make_async_remote_copy(
+                    src_ref=e_own, dst_ref=e_in.at[i - 1], send_sem=e_send.at[0], recv_sem=e_recv.at[0],
+                    device_id=in_group(i)[1], device_id_type=MESH,
+                ).start()
+
         @pl.when(r == 2)
+        def _():
+            learn(2)
+
+        @pl.when(r == 4)
         def _():
             wait_bytes(e_in, e_recv.at[0])
             total = e_own[...]
@@ -219,10 +242,10 @@
     average = e_total / walkers
     lanes = 2 * cols // Z
     for c in range(Z // 2):
-        weighted = done[pl.ds(c, chunks, stride=Z), :] / walkers
-        logs = done[pl.ds(c + Z // 2, chunks, stride=Z), :] / walkers
-        gradient[:, c * lanes : (c + 1) * lanes] = weighted - 2.0 * average * logs
-        log_mean[:, c * lanes : (c + 1) * lanes] = logs
+        weighted = done[pl.ds(c, chunks, stride=Z), :]
+        logs = done[pl.ds(c + Z // 2, chunks, stride=Z), :]
+        sums[:, c * lanes : (c + 1) * lanes] = weighted - 2.0 * average * logs
+        sums[:, cols + c * lanes : cols + (c + 1) * lanes] = logs
 
     for way in range(2):
         base = RIGHT if way == 0 else LEFT
@@ -243,17 +266,16 @@
     chunks = occ // walkers
     rows = walkers
     sizes = (ring, occ, depth, cols, chunks, rows)
-    hbm = pl.BlockSpec(memory_space=pl.ANY)
+    hbm = pl.BlockSpec(memory_space=pltpu.HBM)
     vmem = pl.BlockSpec(memory_space=pltpu.VMEM)
     f32, b16 = jnp.float32, inverse_rows.dtype
     dma = pltpu.SemaphoreType.DMA
     lanes = 2 * cols // Z
-    out = jax.ShapeDtypeStruct((occ // walkers, cols), f32)
-    return pl.pallas_call(
+    sums = pl.pallas_call(
         functools.partial(kernel, sizes),
-        out_shape=(out, out),
-        in_specs=[hbm, hbm, hbm, hbm, pl.BlockSpec(memory_space=pltpu.SMEM)],
-        out_specs=(vmem, vmem),
+        out_shape=jax.ShapeDtypeStruct((chunks, 2 * cols), f32),
+        in_specs=[hbm] * 5,
+        out_specs=vmem,
         scratch_shapes=[
             pltpu.VMEM((2, occ, depth), b16),
             pltpu.VMEM((2, depth // 128, occ, 128), f32),
@@ -271,7 +293,8 @@
             pltpu.VMEM((GROUP - 1, 8, lanes), f32),
             pltpu.VMEM((8, lanes), f32),
             pltpu.VMEM((Z - 1, 8, lanes), f32),
-            dma((4,)),
+            pltpu.SMEM((1,), f32),
+            dma((5,)),
             dma((2, 4)),
             dma((2, 4, chunks)),
             dma,
@@ -280,9 +303,11 @@
             dma((chunks,)),
             dma((2,)),
             dma((2,)),
+            pltpu.SemaphoreType.REGULAR((3,)),
         ],
-        compiler_params=pltpu.CompilerParams(collective_id=0, has_side_effects=True, vmem_limit_bytes=56 * 1024 * 1024),
+        compiler_params=pltpu.CompilerParams(collective_id=0, has_side_effects=True, vmem_limit_bytes=55088 * 1024),
     )(inverse_rows, kinetic_rows, virt_values, virt_laplacians, local_energy)
+    return (sums[:, :cols] / walkers, sums[:, cols:] / walkers)
 
 
 def solution(mesh):

time: 74.5 us -> 71.2 us (0.956)
  local copies, waits for them, and re-layouts: 2.65 us -> 0 us
  Pallas kernels: 70.2 us -> 69.2 us
    unnamed x2 -> x0, local copies, waits for them, and re-layouts: 2.65 us -> none
    pallas_call x1, Pallas kernels: 70.2 us -> 69.2 us  [body(): pl.pallas_call(functools.partial(kernel, sizes), out_shape=jax.ShapeDtype...]
where the time goes in v2:
time: 71.2 us; the launch traced here: 71.1 us
  Pallas kernels  69.2 us (97%)
  between operations  1.29 us (2%)
    pallas_call x1, Pallas kernels, body(): pl.pallas_call(functools.partial(kernel, sizes), out_shape=jax.ShapeDtype...  69.2 us

profile of v2, /device:TPU:1, one launch (start us, length us, event | category | flops | bytes accessed | tf_op | source)
XLA Modules:
  0.0 71.1 jit_solution(10652249041021380747)
XLA Ops:
  1.3 69.2 %shard_map.68 = f32[8,1024]{1,0:T(8,128)S(1)} custom-call(bf16[1,512,256]{2,1,0:T(8,128)(2,1)} %inverse.1, bf16[1,512,256]{2,1,0:T(8,128)(2,1)} %kinetic.1, bf16[1,2048,512]{2,1,0:T(8,128)(2,1)} %values.1, bf16[1,2048,512]{2,1,0:T(8,128)(2,1)} %laplacians.1, f32[1]{0:T(128)S(6)} %copy.7.energy_in), custom_call_target="tpu_custom_call" | custom-call | tf_op jit(solution)/shard_map/pallas_call | solution.py:274
  70.5 0.6 slice_multiply_fusion

commit v3 on v2

v3 whole, which is shorter than its diff:
```python
import functools

import jax
import jax.numpy as jnp
from jax import lax
from jax.experimental import pallas as pl
from jax.experimental.pallas import tpu as pltpu
from jax.sharding import PartitionSpec as P

MESH = pl.DeviceIdType.MESH
X, Z, CORES = 4, 8, 2
GROUP = X * CORES
AHEAD, LAG, FAR_ROUND = 6, 3, 9
PAIR_ROUNDS, PART_ROUNDS, ROW_ROUNDS = 1, 7, 14
OWN, RIGHT, LEFT, FAR = 0, 1, 4, 7


def kernel(sizes, inverse, kinetic, values, laplacians, energy_in, sums, *scratch):
    ring, depth, cols, per_owner, chunks, rows = sizes
    (raw, wide, held, vals, laps, acc, acc_lap, part, pair_in, part_in, row, row_in, done) = scratch[:13]
    (e_own, e_in, e_sum, e_sum_in, energy) = scratch[13:18]
    (load_sem, ring_send, ring_recv, pair_send, pair_recv, part_send, part_recv) = scratch[18:25]
    (row_send, row_recv, e_send, e_recv, known) = scratch[25:]
    walkers = X * Z * CORES
    lanes = 2 * cols // Z

    y = lax.axis_index("virt")
    w = lax.axis_index("walk")
    x, z, core = w // (Z * CORES), (w // CORES) % Z, w % CORES
    group = x * CORES + core
    right, left = lax.rem(y + 1, ring), lax.rem(y + ring - 1, ring)

    def at(x, z, core):
        return {"walk": (x * Z + z) * CORES + core}

    def in_group(i):
        other = lax.rem(group + i, GROUP)
        return at(other // CORES, z, other % CORES)

    def along_x(i):
        other = lax.rem(x + i, X)
        return other, at(other, z, core)

    def along_z(i):
        other = lax.rem(z + i, Z)
        return other, at(x, other, core)

    partner = at(x, z, 1 - core)

    def send(src, dst, send_sem, recv_sem, device):
        return pltpu.make_async_remote_copy(
            src_ref=src, dst_ref=dst, send_sem=send_sem, recv_sem=recv_sem, device_id=device, device_id_type=MESH
        )

    def wait_bytes(ref, sem):
        pltpu.make_async_copy(ref, ref, sem).wait()

    loads = [
        pltpu.make_async_copy(inverse.at[0], raw.at[0], load_sem.at[0]),
        pltpu.make_async_copy(kinetic.at[0], raw.at[1], load_sem.at[1]),
        pltpu.make_async_copy(values.at[0], vals, load_sem.at[2]),
        pltpu.make_async_copy(laplacians.at[0], laps, load_sem.at[3]),
        pltpu.make_async_copy(energy_in, energy, load_sem.at[4]),
    ]
    for load in loads[:2]:
        load.start()

    barrier = pltpu.get_barrier_semaphore()
    near = [along_x(d)[1] for d in (1, X - 1)] + [along_z(d)[1] for d in (1, Z - 1)] + [partner]
    for device in near + [{"virt": right}, {"virt": left}]:
        pl.semaphore_signal(barrier, inc=1, device_id=device, device_id_type=MESH)

    def tell(stage):
        for device in near:
            pl.semaphore_signal(known.at[stage], inc=1, device_id=device, device_id_type=MESH)

    def learn(stage):
        pl.semaphore_wait(known.at[stage], len(near))

    def hop(q, way, step):
        base = RIGHT if way == 0 else LEFT
        if step == 3:
            src, dst = held.at[q, base + 2, way], held.at[q, FAR, way]
        else:
            src = held.at[q, OWN if step == 0 else base + step - 1]
            dst = held.at[q, base + step]
        to = {"virt": right if way == 0 else left}
        return send(src, dst, ring_send.at[way, step], ring_recv.at[way, step, q], to)

    def permute(q):
        for a in range(2):
            for half in range(depth // 128):
                first = per_owner * (q % CORES) + q // CORES
                pieces = [
                    wide[a, half, pl.ds(Z * CORES * per_owner * g + first, Z, stride=CORES * per_owner), :]
                    for g in range(X)
                ]
                held[q, OWN, a, :, half * 128 : (half + 1) * 128] = jnp.concatenate(pieces, axis=0).astype(held.dtype)

    for a in range(2):
        loads[a].wait()
        for half in range(depth // 128):
            wide[a, half] = raw[a, :, half * 128 : (half + 1) * 128].astype(jnp.float32)
    for load in loads[2:]:
        load.start()
    permute(0)
    pl.semaphore_wait(barrier, len(near) + 2)
    for q in range(AHEAD):
        if q:
            permute(q)
        for way in range(2):
            hop(q, way, 0).start()
    tell(0)
    for q in range(AHEAD, chunks):
        permute(q)
    loads[4].wait()
    e_own[...] = jnp.full(e_own.shape, energy[0], jnp.float32)
    for load in loads[2:4]:
        load.wait()

    def accumulate(q, slot, origin, first=False):
        block = pl.ds(pl.multiple_of(origin * depth, depth), depth)
        both = held[q, slot].reshape(2 * rows, depth)
        mine = jnp.dot(both, vals[block, :], preferred_element_type=jnp.float32)
        curved = jnp.dot(both[:rows], laps[block, :], preferred_element_type=jnp.float32)
        if first:
            acc[q] = mine
            acc_lap[q] = curved
        else:
            acc[q] += mine
            acc_lap[q] += curved

    def send_pair(q):
        log_grad = acc[q, :rows]
        kin_part = acc_lap[q] - acc[q, rows:]
        weighted = 2.0 * energy[0] * log_grad - 0.5 * kin_part
        part[q, :, :, :cols] = weighted.reshape(X, Z, cols)
        part[q, :, :, cols:] = log_grad.reshape(X, Z, cols)

        @pl.when(lax.rem(q, CORES) != core)
        def _():
            send(part.at[q], pair_in.at[q], pair_send, pair_recv.at[q], partner).start()

    def send_part(q):
        wait_bytes(pair_in.at[q], pair_recv.at[q])
        part[q] += pair_in[q]
        for i in (2, 1, 3):
            other, device = along_x(i)
            send(part.at[q, other], part_in.at[q, i - 1], part_send, part_recv.at[q], device).start()

    def send_rows(q):
        wait_bytes(part_in.at[q], part_recv.at[q])
        total = part[q, x]
        for i in range(X - 1):
            total = total + part_in[q, i]
        for c in range(Z):
            row[q, pl.ds(c, Z, stride=Z), :] = total[:, c * lanes : (c + 1) * lanes]
        for i in (4, 3, 5, 2, 6, 1, 7):
            other, device = along_z(i)
            src = row.at[q, pl.ds(pl.multiple_of(other * Z, Z), Z)]
            send(src, row_in.at[q, i - 1], row_send, row_recv.at[q], device).start()

    def finish(q):
        wait_bytes(row_in.at[q], row_recv.at[q])
        total = row[q, pl.ds(pl.multiple_of(z * Z, Z), Z)]
        for i in range(Z - 1):
            total = total + row_in[q, i]
        done[pl.ds(pl.multiple_of((q // CORES) * Z, Z), Z), :] = total

    def within(q):
        return jnp.logical_and(q >= 0, q < chunks)

    def when_owner(q, act):
        @pl.when(jnp.logical_and(within(q), lax.rem(q + chunks, CORES) == core))
        def _():
            act(q)

    def one_round(r, carry):
        @pl.when(r + AHEAD < chunks)
        def _():
            for way in range(2):
                hop(r + AHEAD, way, 0).start()

        for step in range(1, 4):
            q = r - LAG * (step - 1)

            @pl.when(within(q))
            def _():
                for way in range(2):
                    hop(q, way, step - 1).wait_recv()
                    hop(q, way, step).start()

        @pl.when(within(r))
        def _():
            accumulate(r, OWN, y, first=True)

        for step in range(1, 4):
            q = r - LAG * (step - 1)

            @pl.when(within(q))
            def _():
                accumulate(q, RIGHT + step - 1, lax.rem(y + ring - step, ring))
                accumulate(q, LEFT + step - 1, lax.rem(y + step, ring))

        far = r - FAR_ROUND

        @pl.when(within(far))
        def _():
            for way in range(2):
                hop(far, way, 3).wait_recv()
            accumulate(far, FAR, lax.rem(y + 4, ring))
            send_pair(far)

        @pl.when(r == 0)
        def _():
            learn(0)
            tell(1)

        @pl.when(r == 1)
        def _():
            learn(1)
            tell(2)
            for i in range(1, GROUP):
                send(e_own, e_in.at[i - 1], e_send.at[0], e_recv.at[0], in_group(i)).start()

        @pl.when(r == 2)
        def _():
            learn(2)

        @pl.when(r == 4)
        def _():
            wait_bytes(e_in, e_recv.at[0])
            total = e_own[...]
            for i in range(GROUP - 1):
                total = total + e_in[i]
            e_sum[...] = total
            for i in range(1, Z):
                send(e_sum, e_sum_in.at[i - 1], e_send.at[1], e_recv.at[1], along_z(i)[1]).start()

        when_owner(far - PAIR_ROUNDS, send_part)
        when_owner(far - PART_ROUNDS, send_rows)
        when_owner(far - ROW_ROUNDS, finish)
        return carry

    lax.fori_loop(0, chunks + FAR_ROUND + ROW_ROUNDS, one_round, 0)

    wait_bytes(e_sum_in, e_recv.at[1])
    e_total = e_sum[...]
    for i in range(Z - 1):
        e_total = e_total + e_sum_in[i]
    average = e_total / walkers
    for c in range(Z // 2):
        weighted = done[pl.ds(c, per_owner, stride=Z), :]
        logs = done[pl.ds(c + Z // 2, per_owner, stride=Z), :]
        sums[:, c * lanes : (c + 1) * lanes] = weighted - 2.0 * average * logs
        sums[:, cols + c * lanes : cols + (c + 1) * lanes] = logs

    for way in range(2):
        base = RIGHT if way == 0 else LEFT
        for step in range(3):
            wait_bytes(held.at[:, base + step], ring_send.at[way, step])
        wait_bytes(held.at[:, FAR, way], ring_send.at[way, 3])
    wait_bytes(pair_in.at[:per_owner], pair_send)
    wait_bytes(part_in.at[:per_owner], part_send)
    wait_bytes(row_in.at[:per_owner], row_send)
    wait_bytes(e_in, e_send.at[0])
    wait_bytes(e_sum_in, e_send.at[1])


def body(inverse_rows, kinetic_rows, virt_values, virt_laplacians, local_energy):
    ring = lax.axis_size("virt")
    walkers = lax.axis_size("walk")
    _, occ, depth = inverse_rows.shape
    _, electrons, cols = virt_values.shape
    per_owner = occ // walkers
    chunks, rows = per_owner * CORES, walkers // CORES
    sizes = (ring, depth, cols, per_owner, chunks, rows)
    hbm = pl.BlockSpec(memory_space=pl.ANY)
    vmem = pl.BlockSpec(memory_space=pltpu.VMEM)
    f32, b16 = jnp.float32, inverse_rows.dtype
    dma = pltpu.SemaphoreType.DMA
    lanes = 2 * cols // Z
    sums = pl.pallas_call(
        functools.partial(kernel, sizes),
        out_shape=jax.ShapeDtypeStruct((per_owner, 2 * cols), f32),
        in_specs=[hbm] * 5,
        out_specs=vmem,
        scratch_shapes=[
            pltpu.VMEM((2, occ, depth), b16),
            pltpu.VMEM((2, depth // 128, occ, 128), f32),
            pltpu.VMEM((chunks, ring, 2, rows, depth), b16),
            pltpu.VMEM((electrons, cols), b16),
            pltpu.VMEM((electrons, cols), b16),
            pltpu.VMEM((chunks, 2 * rows, cols), f32),
            pltpu.VMEM((chunks, rows, cols), f32),
            pltpu.VMEM((chunks, X, Z, 2 * cols), f32),
            pltpu.VMEM((chunks, X, Z, 2 * cols), f32),
            pltpu.VMEM((chunks, X - 1, Z, 2 * cols), f32),
            pltpu.VMEM((chunks, Z * Z, lanes), f32),
            pltpu.VMEM((chunks, Z - 1, Z, lanes), f32),
            pltpu.VMEM((per_owner * Z, lanes), f32),
            pltpu.VMEM((8, lanes), f32),
            pltpu.VMEM((GROUP - 1, 8, lanes), f32),
            pltpu.VMEM((8, lanes), f32),
            pltpu.VMEM((Z - 1, 8, lanes), f32),
            pltpu.SMEM((1,), f32),
            dma((5,)),
            dma((2, 4)),
            dma((2, 4, chunks)),
            dma,
            dma((chunks,)),
            dma,
            dma((chunks,)),
            dma,
            dma((chunks,)),
            dma((2,)),
            dma((2,)),
            pltpu.SemaphoreType.REGULAR((3,)),
        ],
        compiler_params=pltpu.CompilerParams(collective_id=0, has_side_effects=True, vmem_limit_bytes=55088 * 1024),
    )(inverse_rows, kinetic_rows, virt_values, virt_laplacians, local_energy)
    return (sums[:, :cols] / walkers, sums[:, cols:] / walkers)


def solution(mesh):
    placed = (
        P("walk", None, "virt"),
        P("walk", None, "virt"),
        P("walk", None, "virt"),
        P("walk", None, "virt"),
        P("walk"),
    )
    return jax.shard_map(
        body,
        mesh=mesh,
        in_specs=placed,
        out_specs=(P("walk", "virt"), P("walk", "virt")),
        check_vma=False,
    )
```

time: 71.2 us -> 69.5 us (0.976)
  Pallas kernels: 69.2 us -> 67.4 us
    pallas_call x1, Pallas kernels: 69.2 us -> 67.4 us  [body(): pl.pallas_call(functools.partial(kernel, sizes), out_shape=jax.ShapeDtype...]
where the time goes in v3:
time: 69.5 us; the launch traced here: 69.3 us
  Pallas kernels  67.4 us (97%)
  between operations  1.29 us (2%)
    pallas_call x1, Pallas kernels, body(): pl.pallas_call(functools.partial(kernel, sizes), out_shape=jax.ShapeDtype...  67.4 us

profile of v3, /device:TPU:1, one launch (start us, length us, event | category | flops | bytes accessed | tf_op | source)
XLA Modules:
  0.0 69.3 jit_solution(5896427895149031723)
XLA Ops:
  1.3 67.4 %shard_map.68 = f32[8,1024]{1,0:T(8,128)S(1)} custom-call(bf16[1,512,256]{2,1,0:T(8,128)(2,1)} %inverse.1, bf16[1,512,256]{2,1,0:T(8,128)(2,1)} %kinetic.1, bf16[1,2048,512]{2,1,0:T(8,128)(2,1)} %values.1, bf16[1,2048,512]{2,1,0:T(8,128)(2,1)} %laplacians.1, f32[1]{0:T(128)S(6)} %copy.7.energy_in), custom_call_target="tpu_custom_call" | custom-call | tf_op jit(solution)/shard_map/pallas_call | solution.py:283
  68.7 0.6 slice_multiply_fusion

commit v4 on v3

--- a/solution.py
+++ b/solution.py
@@ -11,19 +11,18 @@
 X, Z, CORES = 4, 8, 2
 GROUP = X * CORES
 AHEAD, LAG, FAR_ROUND = 6, 3, 9
-PAIR_ROUNDS, PART_ROUNDS, ROW_ROUNDS = 1, 7, 14
+PAIR_ROUNDS, PART_ROUNDS = 1, 5
+Z_ROUND = 12
 OWN, RIGHT, LEFT, FAR = 0, 1, 4, 7
 
 
 def kernel(sizes, inverse, kinetic, values, laplacians, energy_in, sums, *scratch):
     ring, depth, cols, per_owner, chunks, rows = sizes
-    (raw, wide, held, vals, laps, acc, acc_lap, part, pair_in, part_in, row, row_in, done) = scratch[:13]
-    (e_own, e_in, e_sum, e_sum_in, energy) = scratch[13:18]
-    (load_sem, ring_send, ring_recv, pair_send, pair_recv, part_send, part_recv) = scratch[18:25]
-    (row_send, row_recv, e_send, e_recv, known) = scratch[25:]
+    (raw, held, vals, laps, acc, acc_lap, part, pair_in, part_in, row, row_in) = scratch[:11]
+    (e_own, e_in, e_sum, e_sum_in, energy) = scratch[11:16]
+    (load_sem, ring_send, ring_recv, pair_send, pair_recv, part_send, part_recv) = scratch[16:23]
+    (row_send, row_recv, e_send, e_recv, known, known_z) = scratch[23:]
     walkers = X * Z * CORES
-    lanes = 2 * cols // Z
-
     y = lax.axis_index("virt")
     w = lax.axis_index("walk")
     x, z, core = w // (Z * CORES), (w // CORES) % Z, w % CORES
@@ -66,9 +65,22 @@
         load.start()
 
     barrier = pltpu.get_barrier_semaphore()
-    near = [along_x(d)[1] for d in (1, X - 1)] + [along_z(d)[1] for d in (1, Z - 1)] + [partner]
+    near = [along_x(d)[1] for d in (1, X - 1)] + [partner]
     for device in near + [{"virt": right}, {"virt": left}]:
         pl.semaphore_signal(barrier, inc=1, device_id=device, device_id_type=MESH)
+    for i in range(1, Z):
+        @pl.when(z + i < Z)
+        def _():
+            pl.semaphore_signal(barrier, inc=1, device_id=at(x, z + i, core), device_id_type=MESH)
+
+    def enter():
+        pl.semaphore_wait(barrier, len(near) + 2 + z)
+
+    def greet_lower():
+        for i in range(1, Z):
+            @pl.when(z >= i)
+            def _():
+                pl.semaphore_signal(known_z, inc=1, device_id=at(x, z - i, core), device_id_type=MESH)
 
     def tell(stage):
         for device in near:
@@ -89,28 +101,26 @@
 
     def permute(q):
         for a in range(2):
-            for half in range(depth // 128):
-                first = per_owner * (q % CORES) + q // CORES
-                pieces = [
-                    wide[a, half, pl.ds(Z * CORES * per_owner * g + first, Z, stride=CORES * per_owner), :]
-                    for g in range(X)
-                ]
-                held[q, OWN, a, :, half * 128 : (half + 1) * 128] = jnp.concatenate(pieces, axis=0).astype(held.dtype)
-
-    for a in range(2):
-        loads[a].wait()
-        for half in range(depth // 128):
-            wide[a, half] = raw[a, :, half * 128 : (half + 1) * 128].astype(jnp.float32)
+            pieces = []
+            for g in range(X):
+                first = (g * Z + q // CORES) * CORES * per_owner
+                both = raw[a, first : first + CORES * per_owner, :].astype(jnp.float32)
+                pieces.append(both[(q % CORES) * per_owner : (q % CORES + 1) * per_owner])
+            held[q, OWN, a] = jnp.concatenate(pieces, axis=0).astype(held.dtype)
+
+    for load in loads[:2]:
+        load.wait()
     for load in loads[2:]:
         load.start()
     permute(0)
-    pl.semaphore_wait(barrier, len(near) + 2)
+    enter()
     for q in range(AHEAD):
         if q:
             permute(q)
         for way in range(2):
             hop(q, way, 0).start()
     tell(0)
+    greet_lower()
     for q in range(AHEAD, chunks):
         permute(q)
     loads[4].wait()
@@ -134,8 +144,8 @@
         log_grad = acc[q, :rows]
         kin_part = acc_lap[q] - acc[q, rows:]
         weighted = 2.0 * energy[0] * log_grad - 0.5 * kin_part
-        part[q, :, :, :cols] = weighted.reshape(X, Z, cols)
-        part[q, :, :, cols:] = log_grad.reshape(X, Z, cols)
+        part[q, :, :, :cols] = weighted.reshape(X, per_owner, cols)
+        part[q, :, :, cols:] = log_grad.reshape(X, per_owner, cols)
 
         @pl.when(lax.rem(q, CORES) != core)
         def _():
@@ -153,19 +163,13 @@
         total = part[q, x]
         for i in range(X - 1):
             total = total + part_in[q, i]
-        for c in range(Z):
-            row[q, pl.ds(c, Z, stride=Z), :] = total[:, c * lanes : (c + 1) * lanes]
-        for i in (4, 3, 5, 2, 6, 1, 7):
-            other, device = along_z(i)
-            src = row.at[q, pl.ds(pl.multiple_of(other * Z, Z), Z)]
-            send(src, row_in.at[q, i - 1], row_send, row_recv.at[q], device).start()
-
-    def finish(q):
-        wait_bytes(row_in.at[q], row_recv.at[q])
-        total = row[q, pl.ds(pl.multiple_of(z * Z, Z), Z)]
-        for i in range(Z - 1):
-            total = total + row_in[q, i]
-        done[pl.ds(pl.multiple_of((q // CORES) * Z, Z), Z), :] = total
+        owner = q // CORES
+        row[owner] = total
+
+        @pl.when(owner != z)
+        def _():
+            slot = lax.rem(z - owner + Z - 1, Z)
+            send(row.at[owner], row_in.at[slot], row_send, row_recv, at(x, owner, core)).start()
 
     def within(q):
         return jnp.logical_and(q >= 0, q < chunks)
@@ -211,23 +215,22 @@
             accumulate(far, FAR, lax.rem(y + 4, ring))
             send_pair(far)
 
-        @pl.when(r == 0)
+        @pl.when(r == 1)
         def _():
             learn(0)
             tell(1)
 
-        @pl.when(r == 1)
+        @pl.when(r == 2)
         def _():
             learn(1)
-            tell(2)
             for i in range(1, GROUP):
                 send(e_own, e_in.at[i - 1], e_send.at[0], e_recv.at[0], in_group(i)).start()
 
-        @pl.when(r == 2)
-        def _():
-            learn(2)
-
-        @pl.when(r == 4)
+        @pl.when(jnp.logical_and(r == Z_ROUND, z < Z - 1))
+        def _():
+            pl.semaphore_wait(known_z, Z - 1 - z)
+
+        @pl.when(r == Z_ROUND)
         def _():
             wait_bytes(e_in, e_recv.at[0])
             total = e_own[...]
@@ -239,21 +242,22 @@
 
         when_owner(far - PAIR_ROUNDS, send_part)
         when_owner(far - PART_ROUNDS, send_rows)
-        when_owner(far - ROW_ROUNDS, finish)
         return carry
 
-    lax.fori_loop(0, chunks + FAR_ROUND + ROW_ROUNDS, one_round, 0)
+    lax.fori_loop(0, chunks + FAR_ROUND + PART_ROUNDS, one_round, 0)
 
     wait_bytes(e_sum_in, e_recv.at[1])
-    e_total = e_sum[...]
+    e_total = e_sum[0:1, 0:1]
     for i in range(Z - 1):
-        e_total = e_total + e_sum_in[i]
+        e_total = e_total + e_sum_in[i, 0:1, 0:1]
     average = e_total / walkers
-    for c in range(Z // 2):
-        weighted = done[pl.ds(c, per_owner, stride=Z), :]
-        logs = done[pl.ds(c + Z // 2, per_owner, stride=Z), :]
-        sums[:, c * lanes : (c + 1) * lanes] = weighted - 2.0 * average * logs
-        sums[:, cols + c * lanes : cols + (c + 1) * lanes] = logs
+    wait_bytes(row_in, row_recv)
+    total = row[z]
+    for i in range(Z - 1):
+        total = total + row_in[i]
+    logs = total[:, cols:]
+    sums[:, :cols] = total[:, :cols] - 2.0 * average * logs
+    sums[:, cols:] = logs
 
     for way in range(2):
         base = RIGHT if way == 0 else LEFT
@@ -262,7 +266,7 @@
         wait_bytes(held.at[:, FAR, way], ring_send.at[way, 3])
     wait_bytes(pair_in.at[:per_owner], pair_send)
     wait_bytes(part_in.at[:per_owner], part_send)
-    wait_bytes(row_in.at[:per_owner], row_send)
+    wait_bytes(row_in, row_send)
     wait_bytes(e_in, e_send.at[0])
     wait_bytes(e_sum_in, e_send.at[1])
 
@@ -279,7 +283,7 @@
     vmem = pl.BlockSpec(memory_space=pltpu.VMEM)
     f32, b16 = jnp.float32, inverse_rows.dtype
     dma = pltpu.SemaphoreType.DMA
-    lanes = 2 * cols // Z
+    lanes = 128
     sums = pl.pallas_call(
         functools.partial(kernel, sizes),
         out_shape=jax.ShapeDtypeStruct((per_owner, 2 * cols), f32),
@@ -287,18 +291,16 @@
         out_specs=vmem,
         scratch_shapes=[
             pltpu.VMEM((2, occ, depth), b16),
-            pltpu.VMEM((2, depth // 128, occ, 128), f32),
             pltpu.VMEM((chunks, ring, 2, rows, depth), b16),
             pltpu.VMEM((electrons, cols), b16),
             pltpu.VMEM((electrons, cols), b16),
             pltpu.VMEM((chunks, 2 * rows, cols), f32),
             pltpu.VMEM((chunks, rows, cols), f32),
-            pltpu.VMEM((chunks, X, Z, 2 * cols), f32),
-            pltpu.VMEM((chunks, X, Z, 2 * cols), f32),
-            pltpu.VMEM((chunks, X - 1, Z, 2 * cols), f32),
-            pltpu.VMEM((chunks, Z * Z, lanes), f32),
-            pltpu.VMEM((chunks, Z - 1, Z, lanes), f32),
-            pltpu.VMEM((per_owner * Z, lanes), f32),
+            pltpu.VMEM((chunks, X, per_owner, 2 * cols), f32),
+            pltpu.VMEM((chunks, X, per_owner, 2 * cols), f32),
+            pltpu.VMEM((chunks, X - 1, per_owner, 2 * cols), f32),
+            pltpu.VMEM((Z, per_owner, 2 * cols), f32),
+            pltpu.VMEM((Z - 1, per_owner, 2 * cols), f32),
             pltpu.VMEM((8, lanes), f32),
             pltpu.VMEM((GROUP - 1, 8, lanes), f32),
             pltpu.VMEM((8, lanes), f32),
@@ -312,10 +314,11 @@
             dma,
             dma((chunks,)),
             dma,
-            dma((chunks,)),
+            dma,
             dma((2,)),
             dma((2,)),
-            pltpu.SemaphoreType.REGULAR((3,)),
+            pltpu.SemaphoreType.REGULAR((2,)),
+            pltpu.SemaphoreType.REGULAR,
         ],
         compiler_params=pltpu.CompilerParams(collective_id=0, has_side_effects=True, vmem_limit_bytes=55088 * 1024),
     )(inverse_rows, kinetic_rows, virt_values, virt_laplacians, local_energy)

time: 69.5 us -> 61.4 us (0.88)
  the two profiles are of different devices: /device:TPU:1 before, /device:TPU:449 now
where the time goes in v4:
time: 61.4 us; the launch traced here: 61.2 us
  Pallas kernels  59.3 us (97%)
  between operations  1.29 us (2%)
  other arithmetic  0.62 us (1%)
    pallas_call x1, Pallas kernels, body(): pl.pallas_call(functools.partial(kernel, sizes), out_shape=jax.ShapeDtype...  59.3 us

profile of v4, /device:TPU:449, one launch (start us, length us, event | category | flops | bytes accessed | tf_op | source)
XLA Modules:
  0.0 61.2 jit_solution(6203686147904118189)
XLA Ops:
  1.3 59.3 %shard_map.68 = f32[8,1024]{1,0:T(8,128)S(1)} custom-call(bf16[1,512,256]{2,1,0:T(8,128)(2,1)} %inverse.1, bf16[1,512,256]{2,1,0:T(8,128)(2,1)} %kinetic.1, bf16[1,2048,512]{2,1,0:T(8,128)(2,1)} %values.1, bf16[1,2048,512]{2,1,0:T(8,128)(2,1)} %laplacians.1, f32[1]{0:T(128)S(6)} %copy.7.energy_in), custom_call_target="tpu_custom_call" | custom-call | tf_op jit(solution)/shard_map/pallas_call | solution.py:287
  60.6 0.6 %slice_multiply_fusion = (f32[8,512]{1,0:T(8,128)}, f32[8,512]{1,0:T(8,128)}) fusion(f32[8,1024]{1,0:T(8,128)S(1)} %shard_map.68), kind=kLoop, calls=%fused_computation | loop fusion | flops 8192 | bytes 65536 | tf_op jit(solution)/shard_map/div | solution.py:325
